TPU v7x, 512 devices: a whole 4x4x16 slice. The times are simulated.
512 devices in a mesh: seq: 64 (over z_lo, y, core), dp: 8 (over z_hi, x).
Axes of the slice: x: 4, y: 4, z: 16 (z_hi: 2, z_lo: 8; z = z_hi * 8 + z_lo), core: 2. Of those that a mesh axis runs over, the one named last changes fastest.
Arguments:
- q_raw: bfloat16 [8, 16384, 1024], P('dp', 'seq'), may hold values from -400 to 400
- k_raw: bfloat16 [8, 16384, 512], P('dp', 'seq'), may hold values from -400 to 400
- values: bfloat16 [8, 16384, 512], P('dp', 'seq'), may hold values from -6 to 6
- grad_out: bfloat16 [8, 16384, 1024], P('dp', 'seq'), may hold values from -80 to 80
- q_gain: float32 [256], replicated, may hold values from 0.5 to 7
- k_gain: float32 [256], replicated, may hold values from 0.5 to 7
Outputs:
- grad_q_raw: bfloat16 [8, 16384, 1024], P('dp', 'seq')
- grad_k_raw: bfloat16 [8, 16384, 512], P('dp', 'seq')
- grad_values: bfloat16 [8, 16384, 512], P('dp', 'seq')
- grad_q_gain: float32 [256], replicated
- grad_k_gain: float32 [256], replicated
All inputs are finite; a program needn't handle non-finite values.
Results may differ from a plain program's by a relative error of at most 0.029.
The roundings to bfloat16 on the way count: a program that leaves them out, or rounds other values in their place, can miss the bound.
Values may be sent and summed in bfloat16 or wider, within the bound.
A program may use at most 128 MiB of HBM per device.

v0:
```python
import jax
import jax.numpy as jnp
from jax import lax
from jax.sharding import PartitionSpec as P

WINDOW = 1024
EPS = 1e-06
ROPE_BASE = 10000.0
MASKED = -1e30


def from_behind(array, axis, by):
    count = lax.axis_size(axis)
    pairs = [(i, i + by) for i in range(count) if 0 <= i + by < count]
    return lax.ppermute(array, axis, pairs)


def rope_tables(positions, head_size):
    half_size = head_size // 2
    freqs = jnp.power(ROPE_BASE, -(2.0 * jnp.arange(half_size, dtype=jnp.float32)) / head_size)
    angles = positions.astype(jnp.float32)[:, None] * freqs[None, :]
    return (jnp.cos(angles), jnp.sin(angles))


def norm_rope(raw_in, gain_in, cosine, sine, head_count):
    head_size = gain_in.shape[0]
    row_count = raw_in.shape[0]
    inputs = raw_in.reshape(row_count, head_count, head_size)
    inverse = lax.rsqrt(jnp.mean(inputs * inputs, axis=-1, keepdims=True) + EPS)
    scaled = inputs * inverse * gain_in
    half_size = head_size // 2
    lower = scaled[..., :half_size]
    upper = scaled[..., half_size:]
    cos_rows = cosine[:, None, :]
    sin_rows = sine[:, None, :]
    turned = jnp.concatenate(
        [lower * cos_rows - upper * sin_rows, upper * cos_rows + lower * sin_rows], axis=-1
    )
    return turned.reshape(row_count, head_count * head_size)


def local(q_raw, k_raw, values, grad_out, q_gain, k_gain):
    q_local = q_raw[0]
    k_local = k_raw[0]
    v_local = values[0]
    do_local = grad_out[0]
    rows_here = q_local.shape[0]
    head_size = q_gain.shape[0]
    query_heads = q_local.shape[1] // head_size
    pair_heads = k_local.shape[1] // head_size
    group_size = query_heads // pair_heads
    reach_dev = WINDOW // rows_here
    key_span = WINDOW + rows_here
    score_scale = head_size ** (-0.5)
    first_pos = lax.axis_index("seq") * rows_here
    positions = first_pos + jnp.arange(rows_here, dtype=jnp.int32)
    cosine, sine = rope_tables(positions, head_size)
    q_rot32, q_back = jax.vjp(
        lambda raw_in, gain_in: norm_rope(raw_in, gain_in, cosine, sine, query_heads),
        q_local.astype(jnp.float32),
        q_gain,
    )
    k_rot32, k_back = jax.vjp(
        lambda raw_in, gain_in: norm_rope(raw_in, gain_in, cosine, sine, pair_heads),
        k_local.astype(jnp.float32),
        k_gain,
    )
    q_rot = q_rot32.astype(jnp.bfloat16)
    k_rot = k_rot32.astype(jnp.bfloat16)
    halo_k = []
    halo_v = []
    for offset in range(reach_dev, 0, -1):
        received = from_behind((k_rot, v_local), "seq", offset)
        halo_k.append(received[0])
        halo_v.append(received[1])
    key_rows = jnp.concatenate(halo_k + [k_rot], axis=0)
    value_rows = jnp.concatenate(halo_v + [v_local], axis=0)
    q_heads = q_rot.reshape(rows_here, pair_heads, group_size, head_size)
    k_heads = key_rows.reshape(key_span, pair_heads, head_size)
    v_heads = value_rows.reshape(key_span, pair_heads, head_size)
    do_heads = do_local.reshape(rows_here, pair_heads, group_size, head_size)
    query_idx = jnp.arange(rows_here, dtype=jnp.int32)[:, None]
    key_idx = jnp.arange(key_span, dtype=jnp.int32)[None, :]
    distance = query_idx + WINDOW - key_idx
    visible = (distance >= 0) & (distance < WINDOW) & (key_idx >= WINDOW - first_pos)
    scores = (
        jnp.einsum("tkgd,skd->kgts", q_heads, k_heads, preferred_element_type=jnp.float32)
        * score_scale
    )
    scores = jnp.where(visible, scores, MASKED)
    row_top = jnp.max(scores, axis=-1, keepdims=True)
    row_total = jnp.log(jnp.sum(jnp.exp(scores - row_top), axis=-1, keepdims=True)) + row_top
    weights = jnp.exp(scores - row_total)
    weights_b = weights.astype(jnp.bfloat16)
    dweights = jnp.einsum("tkgd,skd->kgts", do_heads, v_heads, preferred_element_type=jnp.float32)
    row_delta = jnp.sum(weights * dweights, axis=-1, keepdims=True)
    dscores = (weights * (dweights - row_delta) * score_scale).astype(jnp.bfloat16)
    dq_rot = jnp.einsum(
        "kgts,skd->tkgd", dscores, k_heads, preferred_element_type=jnp.float32
    ).reshape(rows_here, query_heads * head_size)
    dk_all = jnp.einsum("kgts,tkgd->skd", dscores, q_heads, preferred_element_type=jnp.float32)
    dv_all = jnp.einsum("kgts,tkgd->skd", weights_b, do_heads, preferred_element_type=jnp.float32)
    dk_own = dk_all[WINDOW:]
    dv_own = dv_all[WINDOW:]
    for offset in range(1, reach_dev + 1):
        low_row = (reach_dev - offset) * rows_here
        sent_k = dk_all[low_row : low_row + rows_here].astype(jnp.bfloat16)
        sent_v = dv_all[low_row : low_row + rows_here].astype(jnp.bfloat16)
        received = from_behind((sent_k, sent_v), "seq", -offset)
        dk_own = dk_own + received[0].astype(jnp.float32)
        dv_own = dv_own + received[1].astype(jnp.float32)
    dk_rot = dk_own.reshape(rows_here, pair_heads * head_size)
    grad_q_local, gain_q_local = q_back(dq_rot)
    grad_k_local, gain_k_local = k_back(dk_rot)
    gain_q_all, gain_k_all = lax.psum((gain_q_local, gain_k_local), ("seq", "dp"))
    grad_v_local = dv_own.reshape(rows_here, pair_heads * head_size).astype(jnp.bfloat16)
    return (
        grad_q_local.astype(jnp.bfloat16)[None],
        grad_k_local.astype(jnp.bfloat16)[None],
        grad_v_local[None],
        gain_q_all,
        gain_k_all,
    )


def solution(mesh):
    return jax.shard_map(
        local,
        mesh=mesh,
        in_specs=(
            P("dp", "seq", None),
            P("dp", "seq", None),
            P("dp", "seq", None),
            P("dp", "seq", None),
            P(),
            P(),
        ),
        out_specs=(P("dp", "seq", None), P("dp", "seq", None), P("dp", "seq", None), P(), P()),
        check_vma=False,
    )
```

profile of v0, /device:TPU:1, one launch (start us, length us, event | category | flops | bytes accessed | tf_op | source)
XLA Modules:
  0.0 258.1 jit_solution(8285778720912913618)
XLA Ops:
  0.7 1.1 copy.101
  3.4 6.4 %collective-permute-start = (bf16[256,512]{0,1:T(8,128)(2,1)S(1)}, bf16[256,512]{0,1:T(8,128)(2,1)}, u32[]{:S(2)}, u32[]{:S(2)}) collective-permute-start(bf16[256,512]{0,1:T(8,128)(2,1)S(1)} %bitcast.80), channel_id=1, source_target_pairs={{0,32},{8,40},{16,48},{24,56},{32,64},{40,72},{48,80},{56,88},{64,... | collective-permute-start | bytes 786440 | tf_op jit(solution)/shard_map/ppermute | solution.py:15
  9.7 4.2 %collective-permute-start.1 = (bf16[256,512]{0,1:T(8,128)(2,1)S(1)}, bf16[256,512]{0,1:T(8,128)(2,1)}, u32[]{:S(2)}, u32[]{:S(2)}) collective-permute-start(bf16[256,512]{0,1:T(8,128)(2,1)S(1)} %bitcast.81), channel_id=1, source_target_pairs={{0,24},{8,32},{16,40},{24,48},{32,56},{40,64},{48,72},{56,80},{64,... | collective-permute-start | bytes 786440 | tf_op jit(solution)/shard_map/ppermute | solution.py:15
  13.9 3.2 %collective-permute-start.2 = (bf16[256,512]{0,1:T(8,128)(2,1)S(1)}, bf16[256,512]{0,1:T(8,128)(2,1)}, u32[]{:S(2)}, u32[]{:S(2)}) collective-permute-start(bf16[256,512]{0,1:T(8,128)(2,1)S(1)} %bitcast.82), channel_id=1, source_target_pairs={{0,16},{8,24},{16,32},{24,40},{32,48},{40,56},{48,64},{56,72},{64,... | collective-permute-start | bytes 786440 | tf_op jit(solution)/shard_map/ppermute | solution.py:15
  17.1 1.9 collective-permute-start.3
  19.2 4.7 %collective-permute-start.4 = (bf16[256,512]{0,1:T(8,128)(2,1)S(1)}, bf16[256,512]{0,1:T(8,128)(2,1)}, u32[]{:S(2)}, u32[]{:S(2)}) collective-permute-start(bf16[256,512]{0,1:T(8,128)(2,1)S(1)} %bitcast.85), channel_id=1, source_target_pairs={{0,32},{8,40},{16,48},{24,56},{32,64},{40,72},{48,80},{56,88},{64,... | collective-permute-start | bytes 786440 | tf_op jit(solution)/shard_map/ppermute | solution.py:15
  25.6 1.1 fusion.20
  27.3 1.2 copy.142
  30.3 3.4 %collective-permute-start.5 = (bf16[256,512]{0,1:T(8,128)(2,1)S(1)}, bf16[256,512]{0,1:T(8,128)(2,1)S(1)}, u32[]{:S(2)}, u32[]{:S(2)}) collective-permute-start(bf16[256,512]{0,1:T(8,128)(2,1)S(1)} %bitcast.87), channel_id=1, source_target_pairs={{0,24},{8,32},{16,40},{24,48},{32,56},{40,64},{48,72},{56,80},{64,... | collective-permute-start | bytes 786440 | tf_op jit(solution)/shard_map/ppermute | solution.py:15
  33.7 1.0 constant_dynamic-update-slice_fusion.4
  34.6 3.9 %collective-permute-start.6 = (bf16[256,512]{0,1:T(8,128)(2,1)S(1)}, bf16[256,512]{0,1:T(8,128)(2,1)}, u32[]{:S(2)}, u32[]{:S(2)}) collective-permute-start(bf16[256,512]{0,1:T(8,128)(2,1)S(1)} %bitcast.88), channel_id=1, source_target_pairs={{0,16},{8,24},{16,32},{24,40},{32,48},{40,56},{48,64},{56,72},{64,... | collective-permute-start | bytes 786440 | tf_op jit(solution)/shard_map/ppermute | solution.py:15
  38.5 1.0 constant_dynamic-update-slice_fusion.3
  39.5 2.2 collective-permute-start.7
  41.7 1.0 constant_dynamic-update-slice_fusion.2
  42.7 1.0 constant_dynamic-update-slice_fusion.1
  43.7 1.0 copy-done.11
  44.7 1.1 copy.110
  46.5 1.1 copy.111
  47.6 1.8 copy.112
  50.9 1.1 copy.113
  52.0 3.0 %fusion.39 = (f32[2,2,256]{2,1,0:T(2,128)S(1)}, f32[2,2,256,1280]{2,3,1,0:T(8,128)S(1)}) fusion(bf16[1280,2,256,1]{0,2,3,1:T(8,128)(2,1)} %bitcast.94, bf16[256,2,2,256]{3,0,2,1:T(8,128)(2,1)} %bitcast.91, pred[256,1280]{0,1:T(8,128)(4,1)} %fusion.20), kind=kOutput, calls=%fused_computation.89 | convolution fusion | flops 675019776 | bytes 7409664 | tf_op jit(solution)/shard_map/tkgd,skd->kgts/dot_general | solution.py:87
  55.7 1.7 copy-done
  57.8 3.2 %fusion.15 = f32[2,1280,256,2]{2,1,3,0:T(8,128)} fusion(bf16[256,2,2,256]{0,3,2,1:T(8,128)(2,1)S(1)} %bitcast.76, bf16[1280,2,256]{2,0,1:T(8,128)(2,1)S(1)} %constant_dynamic-update-slice_fusion.5), kind=kOutput, calls=%fused_computation.20 | convolution fusion | flops 671088640 | bytes 7077888 | tf_op jit(solution)/shard_map/tkgd,skd->kgts/dot_general | solution.py:95
  61.0 10.9 %fusion.6 = f32[2,256,2,256]{3,1,2,0:T(8,128)} fusion(bf16[1280,2,256,1]{0,2,3,1:T(8,128)(2,1)} %bitcast.95, f32[2,1280,256,2]{2,1,3,0:T(8,128)} %fusion.15, f32[2,2,256,1280]{2,3,1,0:T(8,128)} %copy-done, f32[2,2,256]{2,1,0:T(2,128)S(1)} %log_add_fusion), kind=kOutput, calls=%fused_computation.13 | convolution fusion | flops 680265984 | bytes 12849152 | tf_op jit(solution)/shard_map/kgts,skd->tkgd/dot_general | solution.py:98
  71.8 11.7 %fusion.40 = (bf16[1280,2,256]{0,2,1:T(8,128)(2,1)}, f32[1280,2,256]{0,2,1:T(8,128)}) fusion(bf16[256,2,2,256]{3,0,2,1:T(8,128)(2,1)S(1)} %bitcast.92, f32[2,1280,256,2]{2,1,3,0:T(8,128)} %fusion.15, f32[2,2,256,1280]{2,3,1,0:T(8,128)} %copy-done, f32[2,2,256]{2,1,0:T(2,128)S(1)} %log_add_fusion), kind=kOutput, calls=%fused_computation.90 | convolution fusion | flops 680921344 | bytes 14946304 | tf_op jit(solution)/shard_map/kgts,tkgd->skd/dot_general | solution.py:101
  83.6 5.4 %fusion.41 = (bf16[1280,2,256]{0,2,1:T(8,128)(2,1)}, f32[1280,2,256]{0,2,1:T(8,128)}) fusion(bf16[256,2,2,256]{0,3,2,1:T(8,128)(2,1)S(1)} %bitcast.77, f32[2,2,256,1280]{2,3,1,0:T(8,128)} %copy-done, f32[2,2,256]{2,1,0:T(2,128)S(1)} %log_add_fusion), kind=kOutput, calls=%fused_computation.91 | convolution fusion | flops 674365440 | bytes 9703424 | tf_op jit(solution)/shard_map/kgts,tkgd->skd/dot_general | solution.py:102
  89.3 1.0 copy.140
  90.3 1.4 multiply_add_fusion.1
  91.7 1.2 multiply_reduce_fusion
  93.9 2.2 fusion.37
  96.0 1.3 collective-permute-start.11
  97.3 1.3 collective-permute-start.10
  98.6 1.3 collective-permute-start.9
  99.9 3.1 %collective-permute-start.8 = (bf16[256,2,256]{0,2,1:T(8,128)(2,1)}, bf16[256,2,256]{0,2,1:T(8,128)(2,1)}, u32[]{:S(2)}, u32[]{:S(2)}) collective-permute-start(bf16[256,2,256]{0,2,1:T(8,128)(2,1)} %get-tuple-element.40), channel_id=1, source_target_pairs={{8,0},{16,8},{24,16},{32,24},{40,32},{48,40},{56,48},{64,56},{72,6... | collective-permute-start | bytes 786440 | tf_op jit(solution)/shard_map/ppermute | solution.py:15
  103.0 1.6 fusion.21
  104.6 1.2 convert_element_type.124
  105.7 2.1 fusion.36
  107.8 1.3 collective-permute-start.15
  109.1 1.3 collective-permute-start.14
  110.6 1.3 collective-permute-start.13
  111.9 10.3 %collective-permute-done.9 = bf16[256,2,256]{0,2,1:T(8,128)(2,1)} collective-permute-done((bf16[256,2,256]{0,2,1:T(8,128)(2,1)}, bf16[256,2,256]{0,2,1:T(8,128)(2,1)}, u32[]{:S(2)}, u32[]{:S(2)}) %collective-permute-start.9) | collective-permute-done | bytes 262176 | tf_op jit(solution)/shard_map/ppermute | solution.py:15
  122.1 1.9 collective-permute-start.12
  124.0 6.9 %collective-permute-done.8 = bf16[256,2,256]{0,2,1:T(8,128)(2,1)} collective-permute-done((bf16[256,2,256]{0,2,1:T(8,128)(2,1)}, bf16[256,2,256]{0,2,1:T(8,128)(2,1)}, u32[]{:S(2)}, u32[]{:S(2)}) %collective-permute-start.8) | collective-permute-done | bytes 262176 | tf_op jit(solution)/shard_map/ppermute | solution.py:15
  131.0 1.5 fusion.29
  133.7 6.3 %collective-permute-done.13 = bf16[256,2,256]{0,2,1:T(8,128)(2,1)S(1)} collective-permute-done((bf16[256,2,256]{0,2,1:T(8,128)(2,1)S(1)}, bf16[256,2,256]{0,2,1:T(8,128)(2,1)S(1)}, u32[]{:S(2)}, u32[]{:S(2)}) %collective-permute-start.13) | collective-permute-done | bytes 262176 | tf_op jit(solution)/shard_map/ppermute | solution.py:15
  140.0 1.9 collective-permute-done.12
  142.0 1.2 fusion.26
  144.0 114.1 %all-reduce.4 = (f32[256]{0:T(256)}, f32[256]{0:T(256)}) all-reduce(f32[256]{0:T(256)S(1)} %copy-done.15, f32[256]{0:T(256)S(1)} %get-tuple-element.32), channel_id=1, replica_groups=mesh['seq'=64,'dp'=8] {'seq','dp'}, use_global_device_ids=true, to_apply=%region_8.9 | all-reduce | flops 512 | bytes 4096 | tf_op jit(solution)/shard_map/psum | solution.py:115
  (84 shorter events, 12.3 us)
Async XLA Ops:
  0.6 18.4 %copy-start.9 = (bf16[1,256,512]{2,1,0:T(8,128)(2,1)S(1)}, bf16[1,256,512]{2,1,0:T(8,128)(2,1)}, u32[]{:S(2)}) copy-start(bf16[1,256,512]{2,1,0:T(8,128)(2,1)} %param.8) | copy-start | bytes 786436
  0.7 23.5 %copy-start.7 = (bf16[1,256,1024]{2,1,0:T(8,128)(2,1)S(1)}, bf16[1,256,1024]{2,1,0:T(8,128)(2,1)}, u32[]{:S(2)}) copy-start(bf16[1,256,1024]{2,1,0:T(8,128)(2,1)} %param.6) | copy-start | bytes 1572868
  3.2 22.0 %copy-start.12 = (f32[256]{0:T(256)S(1)}, f32[256]{0:T(256)}, u32[]{:S(2)}) copy-start(f32[256]{0:T(256)} %param.10) | copy-start | bytes 3076
  3.4 26.9 %collective-permute-start = (bf16[256,512]{0,1:T(8,128)(2,1)S(1)}, bf16[256,512]{0,1:T(8,128)(2,1)}, u32[]{:S(2)}, u32[]{:S(2)}) collective-permute-start(bf16[256,512]{0,1:T(8,128)(2,1)S(1)} %bitcast.80), channel_id=1, source_target_pairs={{0,32},{8,40},{16,48},{24,56},{32,64},{40,72},{48,80},{56,88},{64,... | collective-permute-start | bytes 786440 | tf_op jit(solution)/shard_map/ppermute | solution.py:15
  9.7 24.9 %collective-permute-start.1 = (bf16[256,512]{0,1:T(8,128)(2,1)S(1)}, bf16[256,512]{0,1:T(8,128)(2,1)}, u32[]{:S(2)}, u32[]{:S(2)}) collective-permute-start(bf16[256,512]{0,1:T(8,128)(2,1)S(1)} %bitcast.81), channel_id=1, source_target_pairs={{0,24},{8,32},{16,40},{24,48},{32,56},{40,64},{48,72},{56,80},{64,... | collective-permute-start | bytes 786440 | tf_op jit(solution)/shard_map/ppermute | solution.py:15
  13.9 25.6 %collective-permute-start.2 = (bf16[256,512]{0,1:T(8,128)(2,1)S(1)}, bf16[256,512]{0,1:T(8,128)(2,1)}, u32[]{:S(2)}, u32[]{:S(2)}) collective-permute-start(bf16[256,512]{0,1:T(8,128)(2,1)S(1)} %bitcast.82), channel_id=1, source_target_pairs={{0,16},{8,24},{16,32},{24,40},{32,48},{40,56},{48,64},{56,72},{64,... | collective-permute-start | bytes 786440 | tf_op jit(solution)/shard_map/ppermute | solution.py:15
  17.1 25.6 %collective-permute-start.3 = (bf16[256,512]{0,1:T(8,128)(2,1)S(1)}, bf16[256,512]{0,1:T(8,128)(2,1)}, u32[]{:S(2)}, u32[]{:S(2)}) collective-permute-start(bf16[256,512]{0,1:T(8,128)(2,1)S(1)} %bitcast.83), channel_id=1, source_target_pairs={{0,8},{8,16},{16,24},{24,32},{32,40},{40,48},{48,56},{56,64},{64,7... | collective-permute-start | bytes 786440 | tf_op jit(solution)/shard_map/ppermute | solution.py:15
  19.2 24.5 %collective-permute-start.4 = (bf16[256,512]{0,1:T(8,128)(2,1)S(1)}, bf16[256,512]{0,1:T(8,128)(2,1)}, u32[]{:S(2)}, u32[]{:S(2)}) collective-permute-start(bf16[256,512]{0,1:T(8,128)(2,1)S(1)} %bitcast.85), channel_id=1, source_target_pairs={{0,32},{8,40},{16,48},{24,56},{32,64},{40,72},{48,80},{56,88},{64,... | collective-permute-start | bytes 786440 | tf_op jit(solution)/shard_map/ppermute | solution.py:15
  24.0 2.7 %copy-start.2 = (f32[256,128]{1,0:T(8,128)}, f32[256,128]{1,0:T(8,128)S(1)}, u32[]{:S(2)}) copy-start(f32[256,128]{1,0:T(8,128)S(1)} %copy.105) | copy-start | bytes 393220
  24.1 2.6 %copy-start.3 = (f32[256,128]{1,0:T(8,128)}, f32[256,128]{1,0:T(8,128)S(1)}, u32[]{:S(2)}) copy-start(f32[256,128]{1,0:T(8,128)S(1)} %copy.104) | copy-start | bytes 393220
  30.3 15.6 %collective-permute-start.5 = (bf16[256,512]{0,1:T(8,128)(2,1)S(1)}, bf16[256,512]{0,1:T(8,128)(2,1)S(1)}, u32[]{:S(2)}, u32[]{:S(2)}) collective-permute-start(bf16[256,512]{0,1:T(8,128)(2,1)S(1)} %bitcast.87), channel_id=1, source_target_pairs={{0,24},{8,32},{16,40},{24,48},{32,56},{40,64},{48,72},{56,80},{64,... | collective-permute-start | bytes 786440 | tf_op jit(solution)/shard_map/ppermute | solution.py:15
  34.6 13.0 %collective-permute-start.6 = (bf16[256,512]{0,1:T(8,128)(2,1)S(1)}, bf16[256,512]{0,1:T(8,128)(2,1)}, u32[]{:S(2)}, u32[]{:S(2)}) collective-permute-start(bf16[256,512]{0,1:T(8,128)(2,1)S(1)} %bitcast.88), channel_id=1, source_target_pairs={{0,16},{8,24},{16,32},{24,40},{32,48},{40,56},{48,64},{56,72},{64,... | collective-permute-start | bytes 786440 | tf_op jit(solution)/shard_map/ppermute | solution.py:15
  39.5 11.4 %collective-permute-start.7 = (bf16[256,512]{0,1:T(8,128)(2,1)S(1)}, bf16[256,512]{0,1:T(8,128)(2,1)}, u32[]{:S(2)}, u32[]{:S(2)}) collective-permute-start(bf16[256,512]{0,1:T(8,128)(2,1)S(1)} %bitcast.89), channel_id=1, source_target_pairs={{0,8},{8,16},{16,24},{24,32},{32,40},{40,48},{48,56},{56,64},{64,7... | collective-permute-start | bytes 786440 | tf_op jit(solution)/shard_map/ppermute | solution.py:15
  43.6 1.1 copy-start.11
  45.8 0.7 copy-start.10
  55.0 2.4 copy-start
  55.0 2.4 copy-start.1
  55.0 2.5 copy-start.6
  55.0 2.8 %copy-start.5 = (bf16[256,2,256]{2,0,1:T(8,128)(2,1)S(1)}, bf16[256,2,256]{2,0,1:T(8,128)(2,1)}, u32[]{:S(2)}) copy-start(bf16[256,2,256]{2,0,1:T(8,128)(2,1)} %copy.114) | copy-start | bytes 786436
  61.0 10.9 %copy-start.8 = (bf16[256,4,256]{2,0,1:T(8,128)(2,1)S(1)}, bf16[256,4,256]{2,0,1:T(8,128)(2,1)}, u32[]{:S(2)}) copy-start(bf16[256,4,256]{2,0,1:T(8,128)(2,1)} %copy.106) | copy-start | bytes 1572868
  83.5 5.4 %copy-start.4 = (f32[2,256,2,256]{3,1,2,0:T(8,128)S(1)}, f32[2,256,2,256]{3,1,2,0:T(8,128)}, u32[]{:S(2)}) copy-start(f32[2,256,2,256]{3,1,2,0:T(8,128)} %fusion.6) | copy-start | bytes 3145732
  89.0 2.7 %copy-start.13 = (f32[256]{0:T(256)S(1)}, f32[256]{0:T(256)}, u32[]{:S(2)}) copy-start(f32[256]{0:T(256)} %param.10) | copy-start | bytes 3076
  96.0 13.1 %collective-permute-start.11 = (bf16[256,2,256]{0,2,1:T(8,128)(2,1)}, bf16[256,2,256]{0,2,1:T(8,128)(2,1)}, u32[]{:S(2)}, u32[]{:S(2)}) collective-permute-start(bf16[256,2,256]{0,2,1:T(8,128)(2,1)} %get-tuple-element.41), channel_id=1, source_target_pairs={{32,0},{40,8},{48,16},{56,24},{64,32},{72,40},{80,48},{88,56},{96,... | collective-permute-start | bytes 786440 | tf_op jit(solution)/shard_map/ppermute | solution.py:15
  97.3 13.3 %collective-permute-start.10 = (bf16[256,2,256]{0,2,1:T(8,128)(2,1)}, bf16[256,2,256]{0,2,1:T(8,128)(2,1)}, u32[]{:S(2)}, u32[]{:S(2)}) collective-permute-start(bf16[256,2,256]{0,2,1:T(8,128)(2,1)} %get-tuple-element.42), channel_id=1, source_target_pairs={{24,0},{32,8},{40,16},{48,24},{56,32},{64,40},{72,48},{80,56},{88,... | collective-permute-start | bytes 786440 | tf_op jit(solution)/shard_map/ppermute | solution.py:15
  98.6 23.5 %collective-permute-start.9 = (bf16[256,2,256]{0,2,1:T(8,128)(2,1)}, bf16[256,2,256]{0,2,1:T(8,128)(2,1)}, u32[]{:S(2)}, u32[]{:S(2)}) collective-permute-start(bf16[256,2,256]{0,2,1:T(8,128)(2,1)} %get-tuple-element.43), channel_id=1, source_target_pairs={{16,0},{24,8},{32,16},{40,24},{48,32},{56,40},{64,48},{72,56},{80,... | collective-permute-start | bytes 786440 | tf_op jit(solution)/shard_map/ppermute | solution.py:15
  99.9 31.0 %collective-permute-start.8 = (bf16[256,2,256]{0,2,1:T(8,128)(2,1)}, bf16[256,2,256]{0,2,1:T(8,128)(2,1)}, u32[]{:S(2)}, u32[]{:S(2)}) collective-permute-start(bf16[256,2,256]{0,2,1:T(8,128)(2,1)} %get-tuple-element.40), channel_id=1, source_target_pairs={{8,0},{16,8},{24,16},{32,24},{40,32},{48,40},{56,48},{64,56},{72,6... | collective-permute-start | bytes 786440 | tf_op jit(solution)/shard_map/ppermute | solution.py:15
  105.7 26.8 %copy-start.14 = (f32[256]{0:T(256)S(1)}, f32[256]{0:T(256)}, u32[]{:S(2)}) copy-start(f32[256]{0:T(256)} %param.11) | copy-start | bytes 3076
  107.8 25.9 %collective-permute-start.15 = (bf16[256,2,256]{0,2,1:T(8,128)(2,1)}, bf16[256,2,256]{0,2,1:T(8,128)(2,1)S(1)}, u32[]{:S(2)}, u32[]{:S(2)}) collective-permute-start(bf16[256,2,256]{0,2,1:T(8,128)(2,1)} %get-tuple-element.37), channel_id=1, source_target_pairs={{32,0},{40,8},{48,16},{56,24},{64,32},{72,40},{80,48},{88,56},{96,... | collective-permute-start | bytes 786440 | tf_op jit(solution)/shard_map/ppermute | solution.py:15
  109.1 24.6 %collective-permute-start.14 = (bf16[256,2,256]{0,2,1:T(8,128)(2,1)}, bf16[256,2,256]{0,2,1:T(8,128)(2,1)S(1)}, u32[]{:S(2)}, u32[]{:S(2)}) collective-permute-start(bf16[256,2,256]{0,2,1:T(8,128)(2,1)} %get-tuple-element.38), channel_id=1, source_target_pairs={{24,0},{32,8},{40,16},{48,24},{56,32},{64,40},{72,48},{80,56},{88,... | collective-permute-start | bytes 786440 | tf_op jit(solution)/shard_map/ppermute | solution.py:15
  110.6 29.5 %collective-permute-start.13 = (bf16[256,2,256]{0,2,1:T(8,128)(2,1)S(1)}, bf16[256,2,256]{0,2,1:T(8,128)(2,1)S(1)}, u32[]{:S(2)}, u32[]{:S(2)}) collective-permute-start(bf16[256,2,256]{0,2,1:T(8,128)(2,1)S(1)} %get-tuple-element.39), channel_id=1, source_target_pairs={{16,0},{24,8},{32,16},{40,24},{48,32},{56,40},{64,48},{72,56},{80,... | collective-permute-start | bytes 786440 | tf_op jit(solution)/shard_map/ppermute | solution.py:15
  122.1 19.9 %collective-permute-start.12 = (bf16[256,2,256]{0,2,1:T(8,128)(2,1)S(1)}, bf16[256,2,256]{0,2,1:T(8,128)(2,1)S(1)}, u32[]{:S(2)}, u32[]{:S(2)}) collective-permute-start(bf16[256,2,256]{0,2,1:T(8,128)(2,1)S(1)} %get-tuple-element.36), channel_id=1, source_target_pairs={{8,0},{16,8},{24,16},{32,24},{40,32},{48,40},{56,48},{64,56},{72,6... | collective-permute-start | bytes 786440 | tf_op jit(solution)/shard_map/ppermute | solution.py:15
  132.5 11.5 %copy-start.15 = (f32[256]{0:T(256)S(1)}, f32[256]{0:T(256)}, u32[]{:S(2)}) copy-start(f32[256]{0:T(256)} %get-tuple-element.30) | copy-start | bytes 3076
where the time goes:
time: 259 us; the launch traced here: 258 us
  blocking collectives  114 us (44%)
  starting transfers between devices  42.5 us (16%)
  matrix products  34.2 us (13%)
  local copies, waits for them, and re-layouts  28.6 us (11%)
  waiting for transfers between devices  25.6 us (10%)
  other arithmetic  11.9 us (5%)
    psum x1, blocking collectives, local(): lax.psum((gain_q_local, gain_k_local), ('seq', 'dp'))  114 us
    ppermute x16, starting transfers between devices, from_behind(): return lax.ppermute(array, axis, pairs)  42.5 us
    ppermute x16, waiting for transfers between devices, from_behind(): return lax.ppermute(array, axis, pairs)  25.6 us
    dot_general x1, matrix products, local(): jnp.einsum('kgts,tkgd->skd', dscores, q_heads, preferred_element_type=jnp...  11.7 us
    unnamed x45, local copies, waits for them, and re-layouts  11.5 us
    dot_general x1, matrix products, local(): jnp.einsum('kgts,skd->tkgd', dscores, k_heads, preferred_element_type=jnp...  10.9 us
    concatenate x6, local copies, waits for them, and re-layouts, local(): value_rows = jnp.concatenate(halo_v + [v_local], axis=0)  5.89 us
    dot_general x1, matrix products, local(): jnp.einsum('kgts,tkgd->skd', weights_b, do_heads, preferred_element_type=...  5.41 us
  transfers between devices with their start and end apart: 16, of which 5 were waited for; matrix products, arithmetic and copies ran while one was open for 9% of the time, Pallas kernels for 0%

commit v1 on v0

--- a/solution.py
+++ b/solution.py
@@ -7,6 +7,7 @@
 EPS = 1e-06
 ROPE_BASE = 10000.0
 MASKED = -1e30
+define_goods_all = lambda body, mesh_ax, chip_axis: lax.psum(lax.psum(body, mesh_ax), chip_axis)
 
 
 def from_behind(array, axis, by):
@@ -112,7 +113,7 @@
     dk_rot = dk_own.reshape(rows_here, pair_heads * head_size)
     grad_q_local, gain_q_local = q_back(dq_rot)
     grad_k_local, gain_k_local = k_back(dk_rot)
-    gain_q_all, gain_k_all = lax.psum((gain_q_local, gain_k_local), ("seq", "dp"))
+    gain_q_all, gain_k_all = define_goods_all((gain_q_local, gain_k_local), "dp", chip_axis="seq")
     grad_v_local = dv_own.reshape(rows_here, pair_heads * head_size).astype(jnp.bfloat16)
     return (
         grad_q_local.astype(jnp.bfloat16)[None],

time: 259 us -> 400 us (1.54)
  blocking collectives: 114 us -> 255 us
    psum x1 -> x2, blocking collectives: 114 us -> 255 us  [the longest x1 211 us: lax.psum(lax.psum(body, mesh_ax), chip_axis)]
  transfers between devices with their start and end apart: 16 -> 16, of which waited for: 5 -> 5; matrix products, arithmetic and copies ran while one was open for 9% -> 6% of each run, Pallas kernels for 0% -> 0%
where the time goes in v1:
time: 400 us; the launch traced here: 399 us
  blocking collectives  255 us (64%)
  starting transfers between devices  42.5 us (11%)
  matrix products  34.2 us (9%)
  local copies, waits for them, and re-layouts  27.8 us (7%)
  waiting for transfers between devices  26.4 us (7%)
  other arithmetic  11.9 us (3%)
    psum x1, blocking collectives, lax.psum(lax.psum(body, mesh_ax), chip_axis)  211 us
    psum x1, blocking collectives, lax.psum(body, mesh_ax)  43.8 us
    ppermute x16, starting transfers between devices, from_behind(): return lax.ppermute(array, axis, pairs)  42.5 us
    ppermute x16, waiting for transfers between devices, from_behind(): return lax.ppermute(array, axis, pairs)  26.4 us
    dot_general x1, matrix products, local(): jnp.einsum('kgts,tkgd->skd', dscores, q_heads, preferred_element_type=jnp...  11.7 us
    unnamed x45, local copies, waits for them, and re-layouts  11.5 us
    dot_general x1, matrix products, local(): jnp.einsum('kgts,skd->tkgd', dscores, k_heads, preferred_element_type=jnp...  10.9 us
  transfers between devices with their start and end apart: 16, of which 5 were waited for; matrix products, arithmetic and copies ran while one was open for 6% of the time, Pallas kernels for 0%

profile of v1, /device:TPU:1, one launch (start us, length us, event | category | flops | bytes accessed | tf_op | source)
XLA Modules:
  0.0 399.2 jit_solution(9458186133957766319)
XLA Ops:
  0.7 1.1 copy.101
  3.4 6.4 %collective-permute-start = (bf16[256,512]{0,1:T(8,128)(2,1)S(1)}, bf16[256,512]{0,1:T(8,128)(2,1)}, u32[]{:S(2)}, u32[]{:S(2)}) collective-permute-start(bf16[256,512]{0,1:T(8,128)(2,1)S(1)} %bitcast.80), channel_id=1, source_target_pairs={{0,32},{8,40},{16,48},{24,56},{32,64},{40,72},{48,80},{56,88},{64,... | collective-permute-start | bytes 786440 | tf_op jit(solution)/shard_map/ppermute | solution.py:16
  9.7 4.2 %collective-permute-start.1 = (bf16[256,512]{0,1:T(8,128)(2,1)S(1)}, bf16[256,512]{0,1:T(8,128)(2,1)}, u32[]{:S(2)}, u32[]{:S(2)}) collective-permute-start(bf16[256,512]{0,1:T(8,128)(2,1)S(1)} %bitcast.81), channel_id=1, source_target_pairs={{0,24},{8,32},{16,40},{24,48},{32,56},{40,64},{48,72},{56,80},{64,... | collective-permute-start | bytes 786440 | tf_op jit(solution)/shard_map/ppermute | solution.py:16
  13.9 3.2 collective-permute-start.2
  17.1 1.9 collective-permute-start.3
  19.2 4.7 %collective-permute-start.4 = (bf16[256,512]{0,1:T(8,128)(2,1)S(1)}, bf16[256,512]{0,1:T(8,128)(2,1)}, u32[]{:S(2)}, u32[]{:S(2)}) collective-permute-start(bf16[256,512]{0,1:T(8,128)(2,1)S(1)} %bitcast.85), channel_id=1, source_target_pairs={{0,32},{8,40},{16,48},{24,56},{32,64},{40,72},{48,80},{56,88},{64,... | collective-permute-start | bytes 786440 | tf_op jit(solution)/shard_map/ppermute | solution.py:16
  25.6 1.1 fusion.20
  27.3 1.2 copy.142
  30.2 3.4 collective-permute-start.5
  33.6 1.0 constant_dynamic-update-slice_fusion.4
  34.6 3.9 collective-permute-start.6
  39.5 2.2 collective-permute-start.7
  41.7 1.0 constant_dynamic-update-slice_fusion.2
  42.7 1.0 constant_dynamic-update-slice_fusion.1
  43.7 1.1 copy-done.11
  44.7 1.1 copy.110
  46.5 1.1 copy.111
  47.6 1.8 copy.112
  50.9 1.1 copy.113
  52.0 3.0 fusion.39
  55.7 1.7 copy-done
  57.8 3.2 fusion.15
  61.0 10.9 %fusion.6 = f32[2,256,2,256]{3,1,2,0:T(8,128)} fusion(bf16[1280,2,256,1]{0,2,3,1:T(8,128)(2,1)} %bitcast.95, f32[2,1280,256,2]{2,1,3,0:T(8,128)} %fusion.15, f32[2,2,256,1280]{2,3,1,0:T(8,128)} %copy-done, f32[2,2,256]{2,1,0:T(2,128)S(1)} %log_add_fusion), kind=kOutput, calls=%fused_computation.13 | convolution fusion | flops 680265984 | bytes 12849152 | tf_op jit(solution)/shard_map/kgts,skd->tkgd/dot_general | solution.py:99
  71.8 11.7 %fusion.40 = (bf16[1280,2,256]{0,2,1:T(8,128)(2,1)}, f32[1280,2,256]{0,2,1:T(8,128)}) fusion(bf16[256,2,2,256]{3,0,2,1:T(8,128)(2,1)S(1)} %bitcast.92, f32[2,1280,256,2]{2,1,3,0:T(8,128)} %fusion.15, f32[2,2,256,1280]{2,3,1,0:T(8,128)} %copy-done, f32[2,2,256]{2,1,0:T(2,128)S(1)} %log_add_fusion), kind=kOutput, calls=%fused_computation.90 | convolution fusion | flops 680921344 | bytes 14946304 | tf_op jit(solution)/shard_map/kgts,tkgd->skd/dot_general | solution.py:102
  83.6 5.4 %fusion.41 = (bf16[1280,2,256]{0,2,1:T(8,128)(2,1)}, f32[1280,2,256]{0,2,1:T(8,128)}) fusion(bf16[256,2,2,256]{0,3,2,1:T(8,128)(2,1)S(1)} %bitcast.77, f32[2,2,256,1280]{2,3,1,0:T(8,128)} %copy-done, f32[2,2,256]{2,1,0:T(2,128)S(1)} %log_add_fusion), kind=kOutput, calls=%fused_computation.91 | convolution fusion | flops 674365440 | bytes 9703424 | tf_op jit(solution)/shard_map/kgts,tkgd->skd/dot_general | solution.py:103
  89.3 1.0 copy.140
  90.3 1.4 multiply_add_fusion.1
  91.7 1.2 multiply_reduce_fusion
  93.9 2.2 fusion.37
  96.0 1.3 collective-permute-start.11
  97.3 1.3 collective-permute-start.10
  98.6 1.3 collective-permute-start.9
  99.9 3.1 collective-permute-start.8
  103.0 1.6 fusion.21
  104.6 1.2 convert_element_type.124
  105.7 1.3 fusion.36
  107.0 1.3 collective-permute-start.15
  108.3 1.3 collective-permute-start.14
  110.6 1.3 collective-permute-start.13
  111.9 11.5 %collective-permute-done.9 = bf16[256,2,256]{0,2,1:T(8,128)(2,1)} collective-permute-done((bf16[256,2,256]{0,2,1:T(8,128)(2,1)}, bf16[256,2,256]{0,2,1:T(8,128)(2,1)}, u32[]{:S(2)}, u32[]{:S(2)}) %collective-permute-start.9) | collective-permute-done | bytes 262176 | tf_op jit(solution)/shard_map/ppermute | solution.py:16
  123.3 1.9 collective-permute-start.12
  125.2 6.9 %collective-permute-done.8 = bf16[256,2,256]{0,2,1:T(8,128)(2,1)} collective-permute-done((bf16[256,2,256]{0,2,1:T(8,128)(2,1)}, bf16[256,2,256]{0,2,1:T(8,128)(2,1)}, u32[]{:S(2)}, u32[]{:S(2)}) %collective-permute-start.8) | collective-permute-done | bytes 262176 | tf_op jit(solution)/shard_map/ppermute | solution.py:16
  132.2 1.5 fusion.29
  135.0 5.1 %collective-permute-done.13 = bf16[256,2,256]{0,2,1:T(8,128)(2,1)S(1)} collective-permute-done((bf16[256,2,256]{0,2,1:T(8,128)(2,1)S(1)}, bf16[256,2,256]{0,2,1:T(8,128)(2,1)S(1)}, u32[]{:S(2)}, u32[]{:S(2)}) %collective-permute-start.13) | collective-permute-done | bytes 262176 | tf_op jit(solution)/shard_map/ppermute | solution.py:16
  140.0 1.9 collective-permute-done.12
  142.0 1.2 fusion.26
  144.0 43.8 %all-reduce.5 = (f32[256]{0:T(256)S(1)}, f32[256]{0:T(256)S(1)}) all-reduce(f32[256]{0:T(256)S(1)} %copy-done.15, f32[256]{0:T(256)S(1)} %get-tuple-element.32), channel_id=1, replica_groups=mesh['seq'=64,'dp'=8] {'dp'}, use_global_device_ids=true, to_apply=%region_8.9 | all-reduce | flops 512 | bytes 4096 | tf_op jit(solution)/shard_map/psum | solution.py:10
  187.9 211.3 %all-reduce.4 = (f32[256]{0:T(256)}, f32[256]{0:T(256)}) all-reduce(f32[256]{0:T(256)S(1)} %get-tuple-element.36, f32[256]{0:T(256)S(1)} %get-tuple-element.37), channel_id=1, replica_groups=mesh['seq'=64,'dp'=8] {'seq'}, use_global_device_ids=true, to_apply=%region_9.10 | all-reduce | flops 512 | bytes 4096 | tf_op jit(solution)/shard_map/psum | solution.py:10
  (85 shorter events, 14.0 us)
Async XLA Ops:
  0.6 18.4 %copy-start.9 = (bf16[1,256,512]{2,1,0:T(8,128)(2,1)S(1)}, bf16[1,256,512]{2,1,0:T(8,128)(2,1)}, u32[]{:S(2)}) copy-start(bf16[1,256,512]{2,1,0:T(8,128)(2,1)} %param.8) | copy-start | bytes 786436
  0.7 23.5 %copy-start.7 = (bf16[1,256,1024]{2,1,0:T(8,128)(2,1)S(1)}, bf16[1,256,1024]{2,1,0:T(8,128)(2,1)}, u32[]{:S(2)}) copy-start(bf16[1,256,1024]{2,1,0:T(8,128)(2,1)} %param.6) | copy-start | bytes 1572868
  3.2 22.0 %copy-start.12 = (f32[256]{0:T(256)S(1)}, f32[256]{0:T(256)}, u32[]{:S(2)}) copy-start(f32[256]{0:T(256)} %param.10) | copy-start | bytes 3076
  3.4 26.9 %collective-permute-start = (bf16[256,512]{0,1:T(8,128)(2,1)S(1)}, bf16[256,512]{0,1:T(8,128)(2,1)}, u32[]{:S(2)}, u32[]{:S(2)}) collective-permute-start(bf16[256,512]{0,1:T(8,128)(2,1)S(1)} %bitcast.80), channel_id=1, source_target_pairs={{0,32},{8,40},{16,48},{24,56},{32,64},{40,72},{48,80},{56,88},{64,... | collective-permute-start | bytes 786440 | tf_op jit(solution)/shard_map/ppermute | solution.py:16
  9.7 24.9 %collective-permute-start.1 = (bf16[256,512]{0,1:T(8,128)(2,1)S(1)}, bf16[256,512]{0,1:T(8,128)(2,1)}, u32[]{:S(2)}, u32[]{:S(2)}) collective-permute-start(bf16[256,512]{0,1:T(8,128)(2,1)S(1)} %bitcast.81), channel_id=1, source_target_pairs={{0,24},{8,32},{16,40},{24,48},{32,56},{40,64},{48,72},{56,80},{64,... | collective-permute-start | bytes 786440 | tf_op jit(solution)/shard_map/ppermute | solution.py:16
  13.9 25.6 %collective-permute-start.2 = (bf16[256,512]{0,1:T(8,128)(2,1)S(1)}, bf16[256,512]{0,1:T(8,128)(2,1)}, u32[]{:S(2)}, u32[]{:S(2)}) collective-permute-start(bf16[256,512]{0,1:T(8,128)(2,1)S(1)} %bitcast.82), channel_id=1, source_target_pairs={{0,16},{8,24},{16,32},{24,40},{32,48},{40,56},{48,64},{56,72},{64,... | collective-permute-start | bytes 786440 | tf_op jit(solution)/shard_map/ppermute | solution.py:16
  17.1 25.5 %collective-permute-start.3 = (bf16[256,512]{0,1:T(8,128)(2,1)S(1)}, bf16[256,512]{0,1:T(8,128)(2,1)}, u32[]{:S(2)}, u32[]{:S(2)}) collective-permute-start(bf16[256,512]{0,1:T(8,128)(2,1)S(1)} %bitcast.83), channel_id=1, source_target_pairs={{0,8},{8,16},{16,24},{24,32},{32,40},{40,48},{48,56},{56,64},{64,7... | collective-permute-start | bytes 786440 | tf_op jit(solution)/shard_map/ppermute | solution.py:16
  19.2 24.5 %collective-permute-start.4 = (bf16[256,512]{0,1:T(8,128)(2,1)S(1)}, bf16[256,512]{0,1:T(8,128)(2,1)}, u32[]{:S(2)}, u32[]{:S(2)}) collective-permute-start(bf16[256,512]{0,1:T(8,128)(2,1)S(1)} %bitcast.85), channel_id=1, source_target_pairs={{0,32},{8,40},{16,48},{24,56},{32,64},{40,72},{48,80},{56,88},{64,... | collective-permute-start | bytes 786440 | tf_op jit(solution)/shard_map/ppermute | solution.py:16
  24.0 2.7 copy-start.2
  24.1 2.6 copy-start.3
  30.2 15.6 %collective-permute-start.5 = (bf16[256,512]{0,1:T(8,128)(2,1)S(1)}, bf16[256,512]{0,1:T(8,128)(2,1)S(1)}, u32[]{:S(2)}, u32[]{:S(2)}) collective-permute-start(bf16[256,512]{0,1:T(8,128)(2,1)S(1)} %bitcast.87), channel_id=1, source_target_pairs={{0,24},{8,32},{16,40},{24,48},{32,56},{40,64},{48,72},{56,80},{64,... | collective-permute-start | bytes 786440 | tf_op jit(solution)/shard_map/ppermute | solution.py:16
  34.6 13.0 %collective-permute-start.6 = (bf16[256,512]{0,1:T(8,128)(2,1)S(1)}, bf16[256,512]{0,1:T(8,128)(2,1)}, u32[]{:S(2)}, u32[]{:S(2)}) collective-permute-start(bf16[256,512]{0,1:T(8,128)(2,1)S(1)} %bitcast.88), channel_id=1, source_target_pairs={{0,16},{8,24},{16,32},{24,40},{32,48},{40,56},{48,64},{56,72},{64,... | collective-permute-start | bytes 786440 | tf_op jit(solution)/shard_map/ppermute | solution.py:16
  39.5 11.4 %collective-permute-start.7 = (bf16[256,512]{0,1:T(8,128)(2,1)S(1)}, bf16[256,512]{0,1:T(8,128)(2,1)}, u32[]{:S(2)}, u32[]{:S(2)}) collective-permute-start(bf16[256,512]{0,1:T(8,128)(2,1)S(1)} %bitcast.89), channel_id=1, source_target_pairs={{0,8},{8,16},{16,24},{24,32},{32,40},{40,48},{48,56},{56,64},{64,7... | collective-permute-start | bytes 786440 | tf_op jit(solution)/shard_map/ppermute | solution.py:16
  43.6 1.1 copy-start.11
  45.8 0.7 copy-start.10
  55.0 2.4 copy-start
  55.0 2.4 copy-start.1
  55.0 2.5 copy-start.6
  55.0 2.8 copy-start.5
  61.0 10.9 %copy-start.8 = (bf16[256,4,256]{2,0,1:T(8,128)(2,1)S(1)}, bf16[256,4,256]{2,0,1:T(8,128)(2,1)}, u32[]{:S(2)}) copy-start(bf16[256,4,256]{2,0,1:T(8,128)(2,1)} %copy.106) | copy-start | bytes 1572868
  83.6 5.4 %copy-start.4 = (f32[2,256,2,256]{3,1,2,0:T(8,128)S(1)}, f32[2,256,2,256]{3,1,2,0:T(8,128)}, u32[]{:S(2)}) copy-start(f32[2,256,2,256]{3,1,2,0:T(8,128)} %fusion.6) | copy-start | bytes 3145732
  89.0 2.7 copy-start.13
  96.0 12.3 %collective-permute-start.11 = (bf16[256,2,256]{0,2,1:T(8,128)(2,1)}, bf16[256,2,256]{0,2,1:T(8,128)(2,1)}, u32[]{:S(2)}, u32[]{:S(2)}) collective-permute-start(bf16[256,2,256]{0,2,1:T(8,128)(2,1)} %get-tuple-element.43), channel_id=1, source_target_pairs={{32,0},{40,8},{48,16},{56,24},{64,32},{72,40},{80,48},{88,56},{96,... | collective-permute-start | bytes 786440 | tf_op jit(solution)/shard_map/ppermute | solution.py:16
  97.3 13.3 %collective-permute-start.10 = (bf16[256,2,256]{0,2,1:T(8,128)(2,1)}, bf16[256,2,256]{0,2,1:T(8,128)(2,1)}, u32[]{:S(2)}, u32[]{:S(2)}) collective-permute-start(bf16[256,2,256]{0,2,1:T(8,128)(2,1)} %get-tuple-element.44), channel_id=1, source_target_pairs={{24,0},{32,8},{40,16},{48,24},{56,32},{64,40},{72,48},{80,56},{88,... | collective-permute-start | bytes 786440 | tf_op jit(solution)/shard_map/ppermute | solution.py:16
  98.6 24.7 %collective-permute-start.9 = (bf16[256,2,256]{0,2,1:T(8,128)(2,1)}, bf16[256,2,256]{0,2,1:T(8,128)(2,1)}, u32[]{:S(2)}, u32[]{:S(2)}) collective-permute-start(bf16[256,2,256]{0,2,1:T(8,128)(2,1)} %get-tuple-element.45), channel_id=1, source_target_pairs={{16,0},{24,8},{32,16},{40,24},{48,32},{56,40},{64,48},{72,56},{80,... | collective-permute-start | bytes 786440 | tf_op jit(solution)/shard_map/ppermute | solution.py:16
  99.9 32.3 %collective-permute-start.8 = (bf16[256,2,256]{0,2,1:T(8,128)(2,1)}, bf16[256,2,256]{0,2,1:T(8,128)(2,1)}, u32[]{:S(2)}, u32[]{:S(2)}) collective-permute-start(bf16[256,2,256]{0,2,1:T(8,128)(2,1)} %get-tuple-element.42), channel_id=1, source_target_pairs={{8,0},{16,8},{24,16},{32,24},{40,32},{48,40},{56,48},{64,56},{72,6... | collective-permute-start | bytes 786440 | tf_op jit(solution)/shard_map/ppermute | solution.py:16
  105.7 28.0 %copy-start.14 = (f32[256]{0:T(256)S(1)}, f32[256]{0:T(256)}, u32[]{:S(2)}) copy-start(f32[256]{0:T(256)} %param.11) | copy-start | bytes 3076
  107.0 28.0 %collective-permute-start.15 = (bf16[256,2,256]{0,2,1:T(8,128)(2,1)S(1)}, bf16[256,2,256]{0,2,1:T(8,128)(2,1)S(1)}, u32[]{:S(2)}, u32[]{:S(2)}) collective-permute-start(bf16[256,2,256]{0,2,1:T(8,128)(2,1)S(1)} %get-tuple-element.39), channel_id=1, source_target_pairs={{32,0},{40,8},{48,16},{56,24},{64,32},{72,40},{80,48},{88,56},{96,... | collective-permute-start | bytes 786440 | tf_op jit(solution)/shard_map/ppermute | solution.py:16
  108.3 26.7 %collective-permute-start.14 = (bf16[256,2,256]{0,2,1:T(8,128)(2,1)S(1)}, bf16[256,2,256]{0,2,1:T(8,128)(2,1)S(1)}, u32[]{:S(2)}, u32[]{:S(2)}) collective-permute-start(bf16[256,2,256]{0,2,1:T(8,128)(2,1)S(1)} %get-tuple-element.40), channel_id=1, source_target_pairs={{24,0},{32,8},{40,16},{48,24},{56,32},{64,40},{72,48},{80,56},{88,... | collective-permute-start | bytes 786440 | tf_op jit(solution)/shard_map/ppermute | solution.py:16
  110.6 29.5 %collective-permute-start.13 = (bf16[256,2,256]{0,2,1:T(8,128)(2,1)S(1)}, bf16[256,2,256]{0,2,1:T(8,128)(2,1)S(1)}, u32[]{:S(2)}, u32[]{:S(2)}) collective-permute-start(bf16[256,2,256]{0,2,1:T(8,128)(2,1)S(1)} %get-tuple-element.41), channel_id=1, source_target_pairs={{16,0},{24,8},{32,16},{40,24},{48,32},{56,40},{64,48},{72,56},{80,... | collective-permute-start | bytes 786440 | tf_op jit(solution)/shard_map/ppermute | solution.py:16
  123.3 18.6 %collective-permute-start.12 = (bf16[256,2,256]{0,2,1:T(8,128)(2,1)S(1)}, bf16[256,2,256]{0,2,1:T(8,128)(2,1)S(1)}, u32[]{:S(2)}, u32[]{:S(2)}) collective-permute-start(bf16[256,2,256]{0,2,1:T(8,128)(2,1)S(1)} %get-tuple-element.38), channel_id=1, source_target_pairs={{8,0},{16,8},{24,16},{32,24},{40,32},{48,40},{56,48},{64,56},{72,6... | collective-permute-start | bytes 786440 | tf_op jit(solution)/shard_map/ppermute | solution.py:16
  133.8 10.3 %copy-start.15 = (f32[256]{0:T(256)S(1)}, f32[256]{0:T(256)}, u32[]{:S(2)}) copy-start(f32[256]{0:T(256)} %get-tuple-element.30) | copy-start | bytes 3076
